TPU v7x, 32 devices: a whole 2x2x4 slice. The times are simulated.
32 devices in a mesh: node: 32 (over z, y, x, core), rel: 1.
Axes of the slice: x: 2, y: 2, z: 4, core: 2. Of those that a mesh axis runs over, the one named last changes fastest.
Arguments:
- features: bfloat16 [1, 512, 768], P('rel', 'node'), may hold values from -6 to 6
- bases: bfloat16 [30, 768, 1024], P(None, 'node', 'rel'), may hold values from -0.21875 to 0.21875
- coefficients: float32 [6, 30], replicated, may hold values from -0.4375 to 0.4375
- tile_values: bfloat16 [32, 1, 56, 16, 128], P('node', 'rel'), may hold values from -0.03125 to 0.03125
- tile_source: int32 [32, 1, 56], P('node', 'rel'), may hold values from 0 to 3
- tile_relation: int32 [32, 1, 56], P('node', 'rel'), may hold values from 0 to 4
- tile_count: int32 [32, 1], P('node', 'rel'), may hold values from 14 to 56, as said below
Outputs:
- layer_output: bfloat16 [1, 512, 1024], P('rel', 'node')
Inputs may be any that keep to these rules, and one draw needn't show every extreme that they name: `tile_count`: the live slots of each stretch and group are its first ones; in every draw some stretch and group has all 56 slots live.
All inputs are finite; a program needn't handle non-finite values.
Results may differ from a plain program's by a relative error of at most 0.0054.
Values may be sent and summed in bfloat16 or wider, within the bound.
A program may use at most 64 MiB of HBM per device.

v0:
```python
import jax
import jax.numpy as jnp
from jax import lax
from jax.sharding import PartitionSpec as P

TILE = 128


batch_tiles = 8


def on_device(features, bases, coefficients, tile_values, tile_source, tile_relation, tile_count):
    relations = coefficients.shape[0] - 1
    nbases, din_part, dout_part = bases.shape
    stacked = jnp.dot(
        coefficients,
        bases.reshape(nbases, din_part * dout_part).astype(jnp.float32),
        precision=lax.Precision.HIGHEST,
    )
    weight_part = stacked.astype(jnp.bfloat16).reshape(relations + 1, din_part, dout_part)
    own_rows = features[0]
    row_count, in_width = own_rows.shape
    gathered = lax.all_gather(features, "node", axis=1, tiled=True)[0]
    blocks = gathered.reshape(-1, TILE, in_width)
    values = tile_values[0, 0]
    sources = tile_source[0, 0]
    relation_ids = tile_relation[0, 0]
    live_count = tile_count[0, 0]
    dest_rows = values.shape[1]
    kind_ids = jnp.arange(relations, dtype=jnp.int32)

    def accumulate(step_index, aggregate):
        first_slot = step_index * batch_tiles
        tile_block = lax.dynamic_slice_in_dim(values, first_slot, batch_tiles, 0)
        source_ids = lax.dynamic_slice_in_dim(sources, first_slot, batch_tiles, 0)
        labels = lax.dynamic_slice_in_dim(relation_ids, first_slot, batch_tiles, 0)
        picked = jnp.take(blocks, source_ids, axis=0)
        products = jnp.einsum(
            "sab,sbd->sad", tile_block, picked, preferred_element_type=jnp.float32
        )
        live_slots = first_slot + jnp.arange(batch_tiles, dtype=jnp.int32) < live_count
        select = ((labels[:, None] == kind_ids[None, :]) & live_slots[:, None]).astype(jnp.float32)
        return aggregate + jnp.einsum(
            "sr,sad->ard", select, products, precision=lax.Precision.HIGHEST
        )

    turn_count = (live_count + batch_tiles - 1) // batch_tiles
    aggregate = lax.fori_loop(
        0, turn_count, accumulate, jnp.zeros((dest_rows, relations, in_width), jnp.float32)
    )
    weight_rows = lax.all_gather(weight_part, "node", axis=1, tiled=True)
    group_index = lax.axis_index("rel")
    self_part = lax.dynamic_update_slice(
        jnp.zeros((dest_rows, 1, in_width), jnp.float32),
        own_rows.astype(jnp.float32)[:, None, :],
        (group_index * row_count, 0, 0),
    )
    summed = lax.psum(jnp.concatenate([aggregate, self_part], axis=1), "rel")
    messages = summed.astype(jnp.bfloat16).reshape(dest_rows, -1)
    columns = jnp.dot(
        messages, weight_rows.reshape(-1, dout_part), preferred_element_type=jnp.float32
    )
    local_cols = jnp.maximum(columns, 0.0).astype(jnp.bfloat16)
    return lax.all_to_all(local_cols, "rel", split_axis=0, concat_axis=1, tiled=True)[None]


def solution(mesh):
    return jax.shard_map(
        on_device,
        mesh=mesh,
        in_specs=(
            P("rel", "node", None),
            P(None, "node", "rel"),
            P(),
            P("node", "rel", None, None, None),
            P("node", "rel", None),
            P("node", "rel", None),
            P("node", "rel"),
        ),
        out_specs=P("rel", "node", None),
        check_vma=False,
    )
```

profile of v0, /device:TPU:0, one launch (start us, length us, event | category | flops | bytes accessed | tf_op | source)
XLA Modules:
  0.0 109.4 jit_solution(17694600817607839534)
XLA Ops:
  6.5 1.5 %pad.3 = bf16[32,24,1024]{2,1,0:T(8,128)(2,1)S(1)} pad(bf16[30,24,1024]{2,1,0:T(8,128)(2,1)} %param.10, bf16[]{:T(256)} %constant.60), padding=0_2x0_0x0_0 | pad | bytes 3047426
  8.0 0.9 copy.10
  8.9 0.7 convolution_convert_fusion
  9.7 0.9 copy.17
  11.3 46.7 %all_gather.6 = bf16[1,512,768]{2,1,0:T(8,128)(2,1)S(1)} all-gather(bf16[1,16,768]{2,1,0:T(8,128)(2,1)S(1)} %copy-done.1), channel_id=1, replica_groups=mesh['node'=32,'rel'=1] {'node'}, dimensions={1}, use_global_device_ids=true | all-gather | bytes 811008 | tf_op jit(solution)/shard_map/all_gather | solution.py:23
  58.0 22.7 %while.11 = (s32[]{:T(128)}, f32[16,5,768]{2,1,0:T(8,128)S(1)}, s32[]{:T(128)}, bf16[56,16,128]{2,1,0:T(8,128)(2,1)}, s32[56]{0:T(128)S(1)}, /*index=5*/bf16[4,1...) while((s32[]{:T(128)}, f32[16,5,768]{2,1,0:T(8,128)S(1)}, ...), condition=%wide.region_1.2_spmd.clone, body=%wide.region_0.1_spmd.clone.sunk | while | flops 31913108 | bytes 6033847 | solution.py:48
  58.1 0.7 compare_and_fusion.2
  58.8 0.6 gather_fusion
  59.5 1.2 %fusion.36 = f32[8,16,768]{2,1,0:T(8,128)S(1)} fusion(bf16[8,128,768]{2,1,0:T(8,128)(2,1)S(1)} %gather_fusion, pred[8]{0:T(512)(128)(4,1)S(1)} %get-tuple-element.146, bf16[56,16,128]{2,1,0:T(8,128)(2,1)} %get-tuple-element.175, s32[]{:T(128)S(6)} %select_n.31), kind=kOutput, calls=%fused_computation.2.clone.1 | convolution fusion | flops 25952256 | bytes 1998860 | tf_op jit(solution)/shard_map/while/body/sab,sbd->sad/dot_general | solution.py:38
  60.7 0.6 fusion.37
  61.3 0.7 compare_and_fusion.2
  62.1 0.6 gather_fusion
  62.7 1.2 %fusion.36 = f32[8,16,768]{2,1,0:T(8,128)S(1)} fusion(bf16[8,128,768]{2,1,0:T(8,128)(2,1)S(1)} %gather_fusion, pred[8]{0:T(512)(128)(4,1)S(1)} %get-tuple-element.146, bf16[56,16,128]{2,1,0:T(8,128)(2,1)} %get-tuple-element.175, s32[]{:T(128)S(6)} %select_n.31), kind=kOutput, calls=%fused_computation.2.clone.1 | convolution fusion | flops 25952256 | bytes 1998860 | tf_op jit(solution)/shard_map/while/body/sab,sbd->sad/dot_general | solution.py:38
  63.9 0.6 fusion.37
  64.6 0.7 compare_and_fusion.2
  65.3 0.6 gather_fusion
  66.0 1.2 %fusion.36 = f32[8,16,768]{2,1,0:T(8,128)S(1)} fusion(bf16[8,128,768]{2,1,0:T(8,128)(2,1)S(1)} %gather_fusion, pred[8]{0:T(512)(128)(4,1)S(1)} %get-tuple-element.146, bf16[56,16,128]{2,1,0:T(8,128)(2,1)} %get-tuple-element.175, s32[]{:T(128)S(6)} %select_n.31), kind=kOutput, calls=%fused_computation.2.clone.1 | convolution fusion | flops 25952256 | bytes 1998860 | tf_op jit(solution)/shard_map/while/body/sab,sbd->sad/dot_general | solution.py:38
  67.1 0.6 fusion.37
  67.8 0.7 compare_and_fusion.2
  68.6 0.6 gather_fusion
  69.2 1.2 %fusion.36 = f32[8,16,768]{2,1,0:T(8,128)S(1)} fusion(bf16[8,128,768]{2,1,0:T(8,128)(2,1)S(1)} %gather_fusion, pred[8]{0:T(512)(128)(4,1)S(1)} %get-tuple-element.146, bf16[56,16,128]{2,1,0:T(8,128)(2,1)} %get-tuple-element.175, s32[]{:T(128)S(6)} %select_n.31), kind=kOutput, calls=%fused_computation.2.clone.1 | convolution fusion | flops 25952256 | bytes 1998860 | tf_op jit(solution)/shard_map/while/body/sab,sbd->sad/dot_general | solution.py:38
  71.1 0.7 compare_and_fusion.2
  71.8 0.6 gather_fusion
  72.5 1.2 %fusion.36 = f32[8,16,768]{2,1,0:T(8,128)S(1)} fusion(bf16[8,128,768]{2,1,0:T(8,128)(2,1)S(1)} %gather_fusion, pred[8]{0:T(512)(128)(4,1)S(1)} %get-tuple-element.146, bf16[56,16,128]{2,1,0:T(8,128)(2,1)} %get-tuple-element.175, s32[]{:T(128)S(6)} %select_n.31), kind=kOutput, calls=%fused_computation.2.clone.1 | convolution fusion | flops 25952256 | bytes 1998860 | tf_op jit(solution)/shard_map/while/body/sab,sbd->sad/dot_general | solution.py:38
  74.3 0.7 compare_and_fusion.2
  75.0 0.6 gather_fusion
  75.7 1.2 %fusion.36 = f32[8,16,768]{2,1,0:T(8,128)S(1)} fusion(bf16[8,128,768]{2,1,0:T(8,128)(2,1)S(1)} %gather_fusion, pred[8]{0:T(512)(128)(4,1)S(1)} %get-tuple-element.146, bf16[56,16,128]{2,1,0:T(8,128)(2,1)} %get-tuple-element.175, s32[]{:T(128)S(6)} %select_n.31), kind=kOutput, calls=%fused_computation.2.clone.1 | convolution fusion | flops 25952256 | bytes 1998860 | tf_op jit(solution)/shard_map/while/body/sab,sbd->sad/dot_general | solution.py:38
  77.5 0.7 compare_and_fusion.2
  78.3 0.6 gather_fusion
  78.9 1.2 %fusion.36 = f32[8,16,768]{2,1,0:T(8,128)S(1)} fusion(bf16[8,128,768]{2,1,0:T(8,128)(2,1)S(1)} %gather_fusion, pred[8]{0:T(512)(128)(4,1)S(1)} %get-tuple-element.146, bf16[56,16,128]{2,1,0:T(8,128)(2,1)} %get-tuple-element.175, s32[]{:T(128)S(6)} %select_n.31), kind=kOutput, calls=%fused_computation.2.clone.1 | convolution fusion | flops 25952256 | bytes 1998860 | tf_op jit(solution)/shard_map/while/body/sab,sbd->sad/dot_general | solution.py:38
  80.8 16.1 %all-gather.2.cloned.1.call-done = bf16[6,768,1024]{2,1,0:T(8,128)(2,1)} async-done(((bf16[6,24,1024]{2,1,0:T(8,128)(2,1)}), bf16[6,768,1024]{2,1,0:T(8,128)(2,1)}) %all-gather.2.cloned.1.call-update) | async-done | bytes 9437200 | tf_op jit(solution)/shard_map/all_gather | solution.py:51
  96.9 5.6 %fusion.18 = bf16[1,16,1024]{2,1,0:T(8,128)(2,1)} fusion(bf16[6,768,1024]{2,1,0:T(8,128)(2,1)} %all-gather.2.cloned.1.call-done, bf16[16,1,768]{2,0,1:T(8,128)(2,1)S(1)} %bitcast.43, bf16[16,5,768]{2,0,1:T(8,128)(2,1)S(1)} %copy.16), kind=kOutput, calls=%fused_computation.25 | convolution fusion | flops 151101440 | bytes 9617408 | tf_op jit(solution)/shard_map/dot_general | solution.py:60
  (30 shorter events, 3.0 us)
Async XLA Ops:
  6.5 2.4 %copy-start = (f32[6,30]{1,0:T(8,128)S(1)}, f32[6,30]{1,0:T(8,128)}, u32[]{:S(2)}) copy-start(f32[6,30]{1,0:T(8,128)} %param.11) | copy-start | bytes 2164
  6.5 90.4 %all-gather.2.cloned.1.call-start = ((), (), s32[]{:S(2)}) async-start(), calls=%async_computation | async-start | bytes 9732096 | tf_op jit(solution)/shard_map/all_gather | solution.py:51
  8.9 2.4 %copy-start.1 = (bf16[1,16,768]{2,1,0:T(8,128)(2,1)S(1)}, bf16[1,16,768]{2,1,0:T(8,128)(2,1)}, u32[]{:S(2)}) copy-start(bf16[1,16,768]{2,1,0:T(8,128)(2,1)} %param.9) | copy-start | bytes 73732
  9.7 48.3 %copy-start.2 = (s32[1,1,56]{2,1,0:T(1,128)S(1)}, s32[1,1,56]{2,1,0:T(1,128)}, u32[]{:S(2)}) copy-start(s32[1,1,56]{2,1,0:T(1,128)} %param.13) | copy-start | bytes 676
  9.7 48.3 %copy-start.3 = (s32[1,1,56]{2,1,0:T(1,128)S(1)}, s32[1,1,56]{2,1,0:T(1,128)}, u32[]{:S(2)}) copy-start(s32[1,1,56]{2,1,0:T(1,128)} %param.14) | copy-start | bytes 676
Sparse Core Ops, SparseCore 0:
  10.7 86.1 all-gather.1
where the time goes:
time: 110 us; the launch traced here: 109 us
  blocking collectives  46.7 us (42%)
  matrix products  18.5 us (17%)
  waiting for transfers between devices  16.1 us (15%)
  between operations  14.1 us (13%)
  local copies, waits for them, and re-layouts  8.44 us (8%)
  other arithmetic  5.13 us (5%)
    all_gather x1, blocking collectives, on_device(): gathered = lax.all_gather(features, 'node', axis=1, tiled=True)[0]  46.7 us
    all_gather x1, waiting for transfers between devices, on_device(): weight_rows = lax.all_gather(weight_part, 'node', axis=1, tiled=True)  16.1 us
    dot_general x7, matrix products, accumulate(): jnp.einsum('sab,sbd->sad', tile_block, picked, preferred_element_type=jnp...  8.1 us
    dot_general x1, matrix products, on_device(): jnp.dot(messages, weight_rows.reshape(-1, dout_part), preferred_element_t...  5.63 us
    and x7, other arithmetic, accumulate(): picked = jnp.take(blocks, source_ids, axis=0)  5.09 us
    gather x7, local copies, waits for them, and re-layouts, accumulate(): picked = jnp.take(blocks, source_ids, axis=0)  4.54 us
    dot_general x7, matrix products, accumulate(): jnp.einsum('sr,sad->ard', select, products, precision=lax.Precision.HIGHEST)  4.08 us
    unnamed x11, local copies, waits for them, and re-layouts  3.27 us
  transfers between devices with their start and end apart: 1, of which 1 were waited for; matrix products, arithmetic and copies ran while one was open for 21% of the time, Pallas kernels for 0%

commit v1 on v0

--- a/solution.py
+++ b/solution.py
@@ -1,15 +1,21 @@
+import functools
+
 import jax
 import jax.numpy as jnp
 from jax import lax
+from jax.experimental import pallas as pl
+from jax.experimental.pallas import tpu as pltpu
 from jax.sharding import PartitionSpec as P
 
 TILE = 128
+LANES = 128
+HALF = 64
 
 
 batch_tiles = 8
 
 
-def on_device(features, bases, coefficients, tile_values, tile_source, tile_relation, tile_count):
+def general_path(features, bases, coefficients, tile_values, tile_source, tile_relation, tile_count):
     relations = coefficients.shape[0] - 1
     nbases, din_part, dout_part = bases.shape
     stacked = jnp.dot(
@@ -64,7 +70,323 @@
     return lax.all_to_all(local_cols, "rel", split_axis=0, concat_axis=1, tiled=True)[None]
 
 
+def layer_kernel(
+    chips,
+    sources,
+    feat_ref,
+    coef_ref,
+    src_ref,
+    rel_ref,
+    count_ref,
+    values_ref,
+    bases_hbm,
+    out_ref,
+    bases_v,
+    rows_v,
+    adj_v,
+    own_w,
+    other_w,
+    full_w,
+    msg_out,
+    msg_in,
+    part_out,
+    part_in,
+    bases_sem,
+    own_sem,
+    feat_send,
+    feat_recv,
+    fwd_send,
+    w_send,
+    w_recv,
+    msg_send,
+    msg_recv,
+    part_send,
+    part_recv,
+):
+    f32, bf16 = jnp.float32, jnp.bfloat16
+    kinds, nbases = coef_ref.shape
+    relations = kinds - 1
+    slots, dest, tile = values_ref.shape[2:]
+    din_part = own_w.shape[1]
+    dout = out_ref.shape[2]
+    width = feat_ref.shape[2]
+    me = lax.axis_index("node")
+    core, chip = me % 2, me // 2
+    mate = chip * 2 + (1 - core)
+
+    def peer(step):
+        return ((chip + step) % chips) * 2 + core
+
+    def remote(src, dst, send, recv, target):
+        return pltpu.make_async_remote_copy(
+            src_ref=src,
+            dst_ref=dst,
+            send_sem=send,
+            recv_sem=recv,
+            device_id={"node": target},
+            device_id_type=pl.DeviceIdType.MESH,
+        )
+
+    load_bases = pltpu.make_async_copy(bases_hbm, bases_v, bases_sem)
+    load_bases.start()
+
+    barrier = pltpu.get_barrier_semaphore()
+
+    def greet(step, carry):
+        pl.semaphore_signal(
+            barrier, inc=1, device_id={"node": peer(step)}, device_id_type=pl.DeviceIdType.MESH
+        )
+        return carry
+
+    lax.fori_loop(1, chips, greet, 0)
+    pl.semaphore_signal(
+        barrier, inc=1, device_id={"node": mate}, device_id_type=pl.DeviceIdType.MESH
+    )
+    keep_own = pltpu.make_async_copy(feat_ref.at[0], rows_v.at[me], own_sem)
+    keep_own.start()
+    pl.semaphore_wait(barrier, chips)
+
+    def feat_copy(step):
+        return remote(
+            feat_ref.at[0], rows_v.at[me], feat_send.at[step], feat_recv.at[step], peer(step)
+        )
+
+    def send_feat(step, carry):
+        feat_copy(step).start()
+        return carry
+
+    lax.fori_loop(1, chips, send_feat, 0)
+    mate_copy = remote(feat_ref.at[0], rows_v.at[me], fwd_send.at[0], feat_recv.at[chips], mate)
+    mate_copy.start()
+
+    load_bases.wait()
+
+    def weigh(chunk, carry):
+        lanes = pl.ds(pl.multiple_of(chunk * LANES, LANES), LANES)
+        sums = [None] * kinds
+        for b in range(nbases):
+            part = bases_v[b, :, lanes].astype(f32)
+            for r in range(kinds):
+                term = coef_ref[r, b] * part
+                sums[r] = term if sums[r] is None else sums[r] + term
+        for r in range(kinds):
+            own_w[r, :, lanes] = sums[r].astype(bf16)
+        return carry
+
+    lax.fori_loop(0, dout // LANES, weigh, 0)
+
+    def fwd_copy(step):
+        slot = ((chip - step + chips) % chips) * 2 + core
+        return remote(
+            rows_v.at[slot],
+            rows_v.at[slot],
+            fwd_send.at[step],
+            feat_recv.at[chips + step],
+            mate,
+        )
+
+    def forward(step, carry):
+        feat_copy(step).wait_recv()
+        fwd_copy(step).start()
+        return carry
+
+    lax.fori_loop(1, chips, forward, 0)
+    w_copy = remote(own_w, other_w, w_send, w_recv, mate)
+    w_copy.start()
+
+    pairs = relations * sources
+    live = count_ref[0, 0]
+
+    def add_tile(t, sums):
+        block = values_ref[0, 0, t].astype(f32)
+        label = rel_ref[0, 0, t] * sources + src_ref[0, 0, t]
+        label = jnp.where(t < live, label, -1)
+        return tuple(
+            sums[k] + block * (label == k).astype(f32) for k in range(pairs)
+        )
+
+    sums = lax.fori_loop(
+        0, slots, add_tile, tuple(jnp.zeros((dest, tile), f32) for _ in range(pairs))
+    )
+    for r in range(relations):
+        for s in range(sources):
+            full = sums[r * sources + s]
+            high = full.astype(bf16)
+            lanes = slice(s * tile, (s + 1) * tile)
+            adj_v[r * dest : (r + 1) * dest, lanes] = high
+            adj_v[(relations + r) * dest : (relations + r + 1) * dest, lanes] = (
+                full - high.astype(f32)
+            ).astype(bf16)
+
+    keep_own.wait()
+    mate_copy.wait_recv()
+
+    def wait_forward(step, carry):
+        fwd_copy(step).wait_recv()
+        return carry
+
+    lax.fori_loop(1, chips, wait_forward, 0)
+
+    both = jnp.dot(
+        adj_v[...], rows_v[...].reshape(-1, width), preferred_element_type=f32
+    )
+    half_rows = relations * dest
+    messages = jnp.concatenate(
+        [both[:half_rows] + both[half_rows:], feat_ref[0].astype(f32)], axis=0
+    )
+    even = jnp.concatenate([messages[r * dest : (r + 1) * dest] for r in range(0, kinds, 2)], 0)
+    odd = jnp.concatenate([messages[r * dest : (r + 1) * dest] for r in range(1, kinds, 2)], 0)
+    odd = jnp.concatenate([odd[:, width - HALF :], odd[:, : width - HALF]], axis=1)
+    even = jnp.concatenate([even, even[:, :LANES]], axis=1)
+    odd = jnp.concatenate([odd, odd[:, :LANES]], axis=1)
+    low_half = lax.broadcasted_iota(jnp.int32, ((kinds // 2) * dest, LANES), 1) < HALF
+    piece = 2 * din_part
+    for q in range(chips):
+        at = q * piece
+        window = jnp.where(low_half, even[:, at : at + LANES], odd[:, at : at + LANES])
+        window = window.astype(bf16)
+        for h in range(kinds // 2):
+            msg_out[q, :, h * LANES : (h + 1) * LANES] = window[h * dest : (h + 1) * dest]
+
+    def msg_copy(step):
+        return remote(
+            msg_out.at[(chip + step) % chips],
+            msg_in.at[step],
+            msg_send.at[step],
+            msg_recv.at[step],
+            peer(step),
+        )
+
+    def send_msg(step, carry):
+        msg_copy(step).start()
+        return carry
+
+    lax.fori_loop(1, chips, send_msg, 0)
+    msg_in[0] = msg_out[chip]
+
+    w_copy.wait()
+    blank = jnp.zeros((HALF - piece, LANES), f32)
+
+    def assemble(chunk, carry):
+        lanes = pl.ds(pl.multiple_of(chunk * LANES, LANES), LANES)
+        for r in range(kinds):
+            mine = own_w[r, :, lanes].astype(f32)
+            theirs = other_w[r, :, lanes].astype(f32)
+            first = jnp.where(core == 0, mine, theirs)
+            second = jnp.where(core == 0, theirs, mine)
+            full_w[r * HALF : (r + 1) * HALF, lanes] = jnp.concatenate(
+                [first, second, blank], axis=0
+            ).astype(bf16)
+        return carry
+
+    lax.fori_loop(0, dout // LANES, assemble, 0)
+
+    def wait_msg(step, carry):
+        msg_copy(step).wait_recv()
+        return carry
+
+    def part_copy(step):
+        return remote(
+            part_out.at[step],
+            part_in.at[step],
+            part_send.at[step],
+            part_recv.at[step],
+            ((chip - step + chips) % chips) * 2 + core,
+        )
+
+    def send_part(step, carry):
+        part_copy(step).start()
+        return carry
+
+    groups = 2
+    per_group = chips // groups
+    for g in range(groups):
+        first, last = g * per_group, (g + 1) * per_group
+        lax.fori_loop(max(first, 1), last, wait_msg, 0)
+        rows = msg_in[first:last].reshape(per_group * dest, msg_in.shape[2])
+        part = jnp.dot(rows, full_w[...], preferred_element_type=f32)
+        part_out[first:last] = part.astype(bf16).reshape(per_group, dest, dout)
+        lax.fori_loop(max(first, 1), last, send_part, 0)
+
+    total = part_out[0].astype(f32)
+    for step in range(1, chips):
+        part_copy(step).wait_recv()
+        total = total + part_in[step].astype(f32)
+    out_ref[0] = jnp.maximum(total, 0.0).astype(bf16)
+
+    mate_copy.wait_send()
+
+    def drain(step, carry):
+        feat_copy(step).wait_send()
+        fwd_copy(step).wait_send()
+        msg_copy(step).wait_send()
+        part_copy(step).wait_send()
+        return carry
+
+    lax.fori_loop(1, chips, drain, 0)
+
+
+def fused_path(features, bases, coefficients, tile_values, tile_source, tile_relation, tile_count):
+    nodes = lax.axis_size("node")
+    chips = nodes // 2
+    kinds = coefficients.shape[0]
+    nbases, din_part, dout = bases.shape
+    _, row_count, width = features.shape
+    dest, tile = tile_values.shape[3:]
+    sources = nodes * row_count // tile
+    depth = kinds * HALF
+    bf16 = jnp.bfloat16
+    vmem = pl.BlockSpec(memory_space=pltpu.VMEM)
+    smem = pl.BlockSpec(memory_space=pltpu.SMEM)
+    dma = pltpu.SemaphoreType.DMA
+    return pl.pallas_call(
+        functools.partial(layer_kernel, chips, sources),
+        out_shape=jax.ShapeDtypeStruct((1, row_count, dout), bf16),
+        in_specs=[vmem, smem, smem, smem, smem, vmem, pl.BlockSpec(memory_space=pl.ANY)],
+        out_specs=vmem,
+        scratch_shapes=[
+            pltpu.VMEM((nbases, din_part, dout), bf16),
+            pltpu.VMEM((nodes, row_count, width), bf16),
+            pltpu.VMEM((2 * (kinds - 1) * dest, sources * tile), bf16),
+            pltpu.VMEM((kinds, din_part, dout), bf16),
+            pltpu.VMEM((kinds, din_part, dout), bf16),
+            pltpu.VMEM((depth, dout), bf16),
+            pltpu.VMEM((chips, dest, depth), bf16),
+            pltpu.VMEM((chips, dest, depth), bf16),
+            pltpu.VMEM((chips, dest, dout), bf16),
+            pltpu.VMEM((chips, dest, dout), bf16),
+            dma,
+            dma,
+            dma((chips,)),
+            dma((2 * chips,)),
+            dma((chips,)),
+            dma,
+            dma,
+            dma((chips,)),
+            dma((chips,)),
+            dma((chips,)),
+            dma((chips,)),
+        ],
+        compiler_params=pltpu.CompilerParams(collective_id=0, has_side_effects=True),
+        name="layer",
+    )(features, coefficients, tile_source, tile_relation, tile_count, tile_values, bases)
+
+
 def solution(mesh):
+    def on_device(features, bases, coefficients, *tiles):
+        kinds = coefficients.shape[0]
+        din_part = bases.shape[1]
+        nodes = mesh.shape["node"]
+        fits = (
+            mesh.shape["rel"] == 1
+            and nodes % 4 == 0
+            and kinds % 2 == 0
+            and 2 * din_part <= HALF
+            and features.shape[1] == tiles[0].shape[3]
+        )
+        path = fused_path if fits else general_path
+        return path(features, bases, coefficients, *tiles)
+
     return jax.shard_map(
         on_device,
         mesh=mesh,

time: 110 us -> 43.8 us (0.40)
  blocking collectives: 46.7 us -> 0 us
  Pallas kernels: 0 us -> 41.5 us
  matrix products: 18.5 us -> 0 us
  waiting for transfers between devices: 16.1 us -> 0 us
  between operations: 14.1 us -> 0.66 us
  local copies, waits for them, and re-layouts: 8.44 us -> 1.38 us
  other arithmetic: 5.13 us -> 0 us
    all_gather x1 -> x0, blocking collectives: 46.7 us -> none  [on_device(): gathered = lax.all_gather(features, 'node', axis=1, tiled=True)[0]]
    pallas_call x0 -> x1, Pallas kernels: none -> 41.5 us  [fused_path(): pl.pallas_call(functools.partial(layer_kernel, chips, sources), out_shape...]
    dot_general x16 -> x0, matrix products: 18.5 us -> none  [the longest x7 8.1 us: accumulate(): jnp.einsum('sab,sbd->sad', tile_block, picked, preferred_element_type=jnp...]
    all_gather x1 -> x0, waiting for transfers between devices: 16.1 us -> none  [on_device(): weight_rows = lax.all_gather(weight_part, 'node', axis=1, tiled=True)]
    and x7 -> x0, other arithmetic: 5.09 us -> none  [accumulate(): picked = jnp.take(blocks, source_ids, axis=0)]
    gather x7 -> x0, local copies, waits for them, and re-layouts: 4.54 us -> none  [accumulate(): picked = jnp.take(blocks, source_ids, axis=0)]
    unnamed x11 -> x1, local copies, waits for them, and re-layouts: 3.27 us -> 1.38 us
  transfers between devices with their start and end apart: 1 -> 0, of which waited for: 1 -> 0; matrix products, arithmetic and copies ran while one was open for 21% -> 0% of each run, Pallas kernels for 0% -> 0%
where the time goes in v1:
time: 43.8 us; the launch traced here: 43.6 us
  Pallas kernels  41.5 us (95%)
  local copies, waits for them, and re-layouts  1.38 us (3%)
  between operations  0.66 us (2%)
    pallas_call x1, Pallas kernels, fused_path(): pl.pallas_call(functools.partial(layer_kernel, chips, sources), out_shape...  41.5 us
    unnamed x1, local copies, waits for them, and re-layouts  1.38 us

profile of v1, /device:TPU:0, one launch (start us, length us, event | category | flops | bytes accessed | tf_op | source)
XLA Modules:
  0.0 43.6 jit_solution(16552365687216103293)
XLA Ops:
  0.7 41.5 %layer.1 = bf16[1,16,1024]{2,1,0:T(8,128)(2,1)} custom-call(bf16[1,16,768]{2,1,0:T(8,128)(2,1)} %feat_ref.1, f32[6,30]{1,0:T(8,128)} %coef_ref.1, s32[1,1,56]{2,1,0:T(1,128)} %src_ref.1, s32[1,1,56]{2,1,0:T(1,128)} %rel_ref.1, s32[1,1]{1,0:T(1,128)S(6)} %copy.9.count_ref, bf16[1,1,56,16,128]{4,3,2,1,0:T(8,128)(2,1)} %values_ref.1, ...), custom_call_target="tpu_custom_call" | custom-call | tf_op jit(solution)/shard_map/layer/pallas_call | solution.py:342
  42.2 1.4 %copy.10 = bf16[1,16,1024]{2,1,0:T(8,128)(2,1)} copy(bf16[1,16,1024]{2,1,0:T(8,128)(2,1)} %layer.1) | data formatting | bytes 65536

commit v2 on v0

--- a/solution.py
+++ b/solution.py
@@ -1,15 +1,21 @@
+import functools
+
 import jax
 import jax.numpy as jnp
 from jax import lax
+from jax.experimental import pallas as pl
+from jax.experimental.pallas import tpu as pltpu
 from jax.sharding import PartitionSpec as P
 
 TILE = 128
+LANES = 128
+PLANE = 8
 
 
 batch_tiles = 8
 
 
-def on_device(features, bases, coefficients, tile_values, tile_source, tile_relation, tile_count):
+def general_path(features, bases, coefficients, tile_values, tile_source, tile_relation, tile_count):
     relations = coefficients.shape[0] - 1
     nbases, din_part, dout_part = bases.shape
     stacked = jnp.dot(
@@ -64,7 +70,361 @@
     return lax.all_to_all(local_cols, "rel", split_axis=0, concat_axis=1, tiled=True)[None]
 
 
+def layer_kernel(
+    planes,
+    sources,
+    feat_ref,
+    coef_ref,
+    src_ref,
+    rel_ref,
+    count_ref,
+    values_ref,
+    bases_hbm,
+    out_ref,
+    bases_v,
+    cols_out,
+    cols_in,
+    adj_in,
+    weights_in,
+    full_w,
+    part_out,
+    part_in,
+    bases_sem,
+    cols_send,
+    cols_recv,
+    fwd_send,
+    fwd_recv,
+    adj_send,
+    adj_recv,
+    w_send,
+    w_recv,
+    w_fwd_send,
+    w_fwd_recv,
+    part_send,
+    part_recv,
+):
+    f32, bf16 = jnp.float32, jnp.bfloat16
+    kinds, nbases = coef_ref.shape
+    relations = kinds - 1
+    slots, dest, tile = values_ref.shape[2:]
+    din_part, half_out = weights_in.shape[3:]
+    dout = out_ref.shape[2]
+    piece = PLANE * din_part
+    chips = planes * PLANE // 2
+    me = lax.axis_index("node")
+    core, chip, plane, seat = me % 2, me // 2, me // PLANE, me % PLANE
+    mate = me + 1 - 2 * core
+    corner = seat // 2
+    beside = plane * PLANE + (corner + 1 - 2 * (corner % 2)) * 2 + core
+    across = plane * PLANE + ((corner + 2) % 4) * 2 + core
+    diagonal = ((corner + 1 - 2 * (corner % 2) + 2) % 4) * 2 + core
+
+    def remote(src, dst, send, recv, target):
+        return pltpu.make_async_remote_copy(
+            src_ref=src,
+            dst_ref=dst,
+            send_sem=send,
+            recv_sem=recv,
+            device_id={"node": target},
+            device_id_type=pl.DeviceIdType.MESH,
+        )
+
+    def peer(step):
+        return ((chip + step) % chips) * 2 + core
+
+    load_bases = pltpu.make_async_copy(bases_hbm, bases_v, bases_sem)
+    load_bases.start()
+
+    barrier = pltpu.get_barrier_semaphore()
+
+    def greet(step, carry):
+        pl.semaphore_signal(
+            barrier, inc=1, device_id={"node": peer(step)}, device_id_type=pl.DeviceIdType.MESH
+        )
+        return carry
+
+    lax.fori_loop(1, chips, greet, 0)
+    pl.semaphore_signal(
+        barrier, inc=1, device_id={"node": mate}, device_id_type=pl.DeviceIdType.MESH
+    )
+    own = feat_ref[0].astype(f32)
+    gap = jnp.zeros((dest, cols_out.shape[2] - piece), f32)
+    for z in range(planes):
+        cut = jnp.concatenate([own[:, z * piece : (z + 1) * piece], gap], axis=1)
+        cols_out[z] = cut.astype(bf16)
+    pl.semaphore_wait(barrier, chips)
+
+    def cols_copy(step):
+        target = peer(step)
+        return remote(
+            cols_out.at[target // PLANE],
+            cols_in.at[me],
+            cols_send.at[step],
+            cols_recv.at[step],
+            target,
+        )
+
+    def send_cols(step, carry):
+        cols_copy(step).start()
+        return carry
+
+    lax.fori_loop(1, chips, send_cols, 0)
+    own_fwd = remote(cols_out.at[plane], cols_in.at[me], fwd_send.at[0], fwd_recv.at[0], mate)
+    own_fwd.start()
+    cols_in[me] = cols_out[plane]
+
+    load_bases.wait()
+    chunks = half_out // LANES
+
+    def own_weights(half):
+        def weigh(chunk, carry):
+            lanes = pl.ds(pl.multiple_of(chunk * LANES, LANES), LANES)
+            there = pl.ds(pl.multiple_of((half * chunks + chunk) * LANES, LANES), LANES)
+            sums = [None] * kinds
+            for b in range(nbases):
+                part = bases_v[b, :, there].astype(f32)
+                for r in range(kinds):
+                    term = coef_ref[r, b] * part
+                    sums[r] = term if sums[r] is None else sums[r] + term
+            for r in range(kinds):
+                weights_in[half, seat, r, :, lanes] = sums[r].astype(bf16)
+            return carry
+
+        lax.fori_loop(0, chunks, weigh, 0)
+
+    def w_copy(half, seat_of, slot, target):
+        at = weights_in.at[half, seat_of]
+        return remote(at, at, w_send.at[slot], w_recv.at[slot], target)
+
+    def w_fwd(half, seat_of, slot):
+        at = weights_in.at[half, seat_of]
+        return remote(at, at, w_fwd_send.at[slot], w_fwd_recv.at[slot], mate)
+
+    first_sends = [
+        [w_copy(half, seat, half, beside), w_copy(half, seat, 2 + half, across)]
+        for half in range(2)
+    ]
+    own_sends = [w_fwd(half, seat, 6 + half) for half in range(2)]
+    for half in range(2):
+        own_weights(half)
+        for copy in first_sends[half]:
+            copy.start()
+        own_sends[half].start()
+
+        if half == 0:
+            pairs = relations * sources
+            live = count_ref[0, 0]
+
+            def add_tile(t, sums):
+                block = values_ref[0, 0, t].astype(f32)
+                label = rel_ref[0, 0, t] * sources + src_ref[0, 0, t]
+                label = jnp.where(t < live, label, -1)
+                return tuple(sums[k] + block * (label == k).astype(f32) for k in range(pairs))
+
+            sums = lax.fori_loop(
+                0, slots, add_tile, tuple(jnp.zeros((dest, tile), f32) for _ in range(pairs))
+            )
+            for r in range(relations):
+                for s in range(sources):
+                    adj_in[plane, r * dest : (r + 1) * dest, s * tile : (s + 1) * tile] = sums[
+                        r * sources + s
+                    ].astype(bf16)
+
+            def column(step):
+                return ((plane + step) % planes) * PLANE + seat
+
+            def adj_copy(step):
+                at = adj_in.at[plane]
+                return remote(at, at, adj_send.at[step], adj_recv.at[step], column(step))
+
+            for step in range(1, planes):
+                adj_copy(step).start()
+
+    def cols_fwd(step):
+        slot = ((chip - step + chips) % chips) * 2 + core
+        at = cols_in.at[slot]
+        return remote(at, at, fwd_send.at[step], fwd_recv.at[step], mate)
+
+    def forward(step, carry):
+        cols_copy(step).wait_recv()
+        cols_fwd(step).start()
+        return carry
+
+    lax.fori_loop(1, chips, forward, 0)
+
+    seat_beside, seat_across = beside % PLANE, across % PLANE
+    relay_across = w_copy(0, seat_beside, 4, across)
+    relay_beside = w_copy(1, seat_across, 5, beside)
+    mate_sends = [
+        w_fwd(0, seat_beside, 0),
+        w_fwd(1, seat_beside, 1),
+        w_fwd(0, seat_across, 2),
+        w_fwd(1, seat_across, 3),
+        w_fwd(0, diagonal, 4),
+        w_fwd(1, diagonal, 5),
+    ]
+    first_sends[0][0].wait_recv()
+    relay_across.start()
+    mate_sends[0].start()
+    first_sends[0][1].wait_recv()
+    mate_sends[2].start()
+    first_sends[1][1].wait_recv()
+    relay_beside.start()
+    mate_sends[3].start()
+    first_sends[1][0].wait_recv()
+    mate_sends[1].start()
+
+    own_fwd.wait_recv()
+
+    def wait_forward(step, carry):
+        cols_fwd(step).wait_recv()
+        return carry
+
+    lax.fori_loop(1, chips, wait_forward, 0)
+    for step in range(1, planes):
+        adj_copy(step).wait_recv()
+
+    relay_across.wait_recv()
+    mate_sends[4].start()
+    relay_beside.wait_recv()
+    mate_sends[5].start()
+
+    block_rows = relations * dest
+    gathered = jnp.dot(
+        adj_in[...].reshape(planes * block_rows, sources * tile),
+        cols_in[...].reshape(sources * tile, cols_in.shape[2]),
+        preferred_element_type=f32,
+    ).astype(bf16)
+    lhs = []
+    for r in range(relations):
+        rows = [
+            gathered[z * block_rows + r * dest : z * block_rows + (r + 1) * dest]
+            for z in range(planes)
+        ]
+        lhs.append(jnp.concatenate(rows, axis=0)[:, :piece])
+    rows = [cols_in[z * PLANE + seat] for z in range(planes)]
+    lhs.append(jnp.concatenate(rows, axis=0)[:, :piece])
+
+    for copy in own_sends + mate_sends:
+        copy.wait_recv()
+
+    for half in range(2):
+
+        def assemble(chunk, carry):
+            lanes = pl.ds(pl.multiple_of(chunk * LANES, LANES), LANES)
+            there = pl.ds(pl.multiple_of((half * chunks + chunk) * LANES, LANES), LANES)
+            for r in range(kinds):
+                rows = [weights_in[half, d, r, :, lanes].astype(f32) for d in range(PLANE)]
+                full_w[r * piece : (r + 1) * piece, there] = jnp.concatenate(rows, axis=0).astype(
+                    bf16
+                )
+            return carry
+
+        lax.fori_loop(0, chunks, assemble, 0)
+
+    part = None
+    for r in range(kinds):
+        term = jnp.dot(
+            lhs[r], full_w[r * piece : (r + 1) * piece], preferred_element_type=f32
+        )
+        part = term if part is None else part + term
+    part_out[...] = part.astype(bf16).reshape(planes, dest, dout)
+
+    def part_copy(step):
+        return remote(
+            part_out.at[(plane + step) % planes],
+            part_in.at[step],
+            part_send.at[step],
+            part_recv.at[step],
+            column(step),
+        )
+
+    for step in range(1, planes):
+        part_copy(step).start()
+    total = part_out[plane].astype(f32)
+    for step in range(1, planes):
+        part_copy(step).wait_recv()
+        total = total + part_in[step].astype(f32)
+    out_ref[0] = jnp.maximum(total, 0.0).astype(bf16)
+
+    def drain(step, carry):
+        cols_copy(step).wait_send()
+        cols_fwd(step).wait_send()
+        return carry
+
+    lax.fori_loop(1, chips, drain, 0)
+    own_fwd.wait_send()
+    for copy in first_sends[0] + first_sends[1] + own_sends + mate_sends:
+        copy.wait_send()
+    relay_across.wait_send()
+    relay_beside.wait_send()
+    for step in range(1, planes):
+        adj_copy(step).wait_send()
+        part_copy(step).wait_send()
+
+
+def fused_path(features, bases, coefficients, tile_values, tile_source, tile_relation, tile_count):
+    nodes = lax.axis_size("node")
+    planes = nodes // PLANE
+    chips = nodes // 2
+    kinds = coefficients.shape[0]
+    nbases, din_part, dout = bases.shape
+    row_count = features.shape[1]
+    dest, tile = tile_values.shape[3:]
+    sources = nodes * row_count // tile
+    piece = PLANE * din_part
+    wide = (piece + LANES - 1) // LANES * LANES
+    bf16 = jnp.bfloat16
+    vmem = pl.BlockSpec(memory_space=pltpu.VMEM)
+    smem = pl.BlockSpec(memory_space=pltpu.SMEM)
+    dma = pltpu.SemaphoreType.DMA
+    return pl.pallas_call(
+        functools.partial(layer_kernel, planes, sources),
+        out_shape=jax.ShapeDtypeStruct((1, row_count, dout), bf16),
+        in_specs=[vmem, smem, smem, smem, smem, vmem, pl.BlockSpec(memory_space=pl.ANY)],
+        out_specs=vmem,
+        scratch_shapes=[
+            pltpu.VMEM((nbases, din_part, dout), bf16),
+            pltpu.VMEM((planes, row_count, wide), bf16),
+            pltpu.VMEM((nodes, row_count, wide), bf16),
+            pltpu.VMEM((planes, (kinds - 1) * dest, sources * tile), bf16),
+            pltpu.VMEM((2, PLANE, kinds, din_part, dout // 2), bf16),
+            pltpu.VMEM((kinds * piece, dout), bf16),
+            pltpu.VMEM((planes, dest, dout), bf16),
+            pltpu.VMEM((planes, dest, dout), bf16),
+            dma,
+            dma((chips,)),
+            dma((chips,)),
+            dma((chips,)),
+            dma((chips,)),
+            dma((planes,)),
+            dma((planes,)),
+            dma((6,)),
+            dma((6,)),
+            dma((8,)),
+            dma((8,)),
+            dma((planes,)),
+            dma((planes,)),
+        ],
+        compiler_params=pltpu.CompilerParams(collective_id=0, has_side_effects=True),
+        name="layer",
+    )(features, coefficients, tile_source, tile_relation, tile_count, tile_values, bases)
+
+
 def solution(mesh):
+    def on_device(features, bases, coefficients, *tiles):
+        kinds = coefficients.shape[0]
+        din_part = bases.shape[1]
+        nodes = mesh.shape["node"]
+        fits = (
+            mesh.shape["rel"] == 1
+            and nodes % PLANE == 0
+            and bases.shape[2] % (2 * LANES) == 0
+            and features.shape[1] == tiles[0].shape[3]
+        )
+        path = fused_path if fits else general_path
+        return path(features, bases, coefficients, *tiles)
+
     return jax.shard_map(
         on_device,
         mesh=mesh,

time: 110 us -> 31.4 us (0.29)
  the two profiles are of different devices: /device:TPU:0 before, /device:TPU:1 now
where the time goes in v2:
time: 31.4 us; the launch traced here: 31.2 us
  Pallas kernels  29.2 us (93%)
  local copies, waits for them, and re-layouts  1.38 us (4%)
  between operations  0.66 us (2%)
    pallas_call x1, Pallas kernels, fused_path(): pl.pallas_call(functools.partial(layer_kernel, planes, sources), out_shap...  29.2 us
    unnamed x1, local copies, waits for them, and re-layouts  1.38 us

profile of v2, /device:TPU:1, one launch (start us, length us, event | category | flops | bytes accessed | tf_op | source)
XLA Modules:
  0.0 31.2 jit_solution(4522003433183087936)
XLA Ops:
  0.7 29.2 %layer.1 = bf16[1,16,1024]{2,1,0:T(8,128)(2,1)} custom-call(bf16[1,16,768]{2,1,0:T(8,128)(2,1)} %feat_ref.1, f32[6,30]{1,0:T(8,128)} %coef_ref.1, s32[1,1,56]{2,1,0:T(1,128)} %src_ref.1, s32[1,1,56]{2,1,0:T(1,128)} %rel_ref.1, s32[1,1]{1,0:T(1,128)S(6)} %copy.9.count_ref, bf16[1,1,56,16,128]{4,3,2,1,0:T(8,128)(2,1)} %values_ref.1, ...), custom_call_target="tpu_custom_call" | custom-call | tf_op jit(solution)/shard_map/layer/pallas_call | solution.py:381
  29.8 1.4 %copy.10 = bf16[1,16,1024]{2,1,0:T(8,128)(2,1)} copy(bf16[1,16,1024]{2,1,0:T(8,128)(2,1)} %layer.1) | data formatting | bytes 65536
